TPU v7x, 32 devices: a whole 2x2x4 slice. The times are simulated.
32 devices in a mesh: groups: 2 (over x), seq: 16 (over z, y, core).
Axes of the slice: x: 2, y: 2, z: 4, core: 2. Of those that a mesh axis runs over, the one named last changes fastest.
Arguments:
- signal: bfloat16 [16384, 2048], P(('groups', 'seq')), parts along dimension 0, may hold values from -6 to 6
- gate_input: bfloat16 [16384, 2048], P(('groups', 'seq')), parts along dimension 0, may hold values from -6 to 6
- cotangent: bfloat16 [16384, 2048], P(('groups', 'seq')), parts along dimension 0, may hold values from -6 to 6
- block_factor: bfloat16 [512, 512], replicated, may hold values from -0.25 to 0.25
- cross_factor: bfloat16 [512, 16, 16], P('seq'), may hold values from -1.5 to 1.5
- order_table: int32 [512], replicated, may hold values from 0 to 511, each once
Outputs:
- grad_signal: bfloat16 [16384, 2048], P(('groups', 'seq')), parts along dimension 0
- grad_gate: bfloat16 [16384, 2048], P(('groups', 'seq')), parts along dimension 0
- grad_block: float32 [1024, 512], P('groups'), parts along dimension 0
- grad_cross: float32 [512, 32, 16], P('seq', 'groups'), parts along dimension 1
There are 2 independent parts, one for each index of `groups`. A program takes and returns all parts, laid end to end along the dimension named above; an argument that names none is the same for every part. Nothing has to cross between parts.
Inputs may be any that keep to these rules, and one draw needn't show every extreme that they name: order_table holds every number of 0 to 511 exactly once.
All inputs are finite; a program needn't handle non-finite values.
Results may differ from a plain program's by a relative error of at most 0.0057.
Values may be sent and summed in bfloat16 or wider, within the bound.
A program may use at most 64 MiB of HBM per device.

v0:
```python
import math
import jax
import jax.numpy as jnp
from jax import lax
from jax.sharding import PartitionSpec as P


def per_device(signal, gate_input, cotangent, block_factor, cross_factor, order_table):
    f32 = jnp.float32
    bf16 = jnp.bfloat16
    count = lax.axis_size("seq")
    width = signal.shape[1]
    permuted = jnp.take(signal, order_table, axis=0)
    mixed = jnp.dot(block_factor, permuted, preferred_element_type=f32).astype(bf16)
    gate_grad = (cotangent.astype(f32) * gate_input.astype(f32)).astype(bf16)
    spread_mixed = lax.all_to_all(mixed[None], "seq", split_axis=1, concat_axis=0, tiled=True)
    spread_grad = lax.all_to_all(gate_grad[None], "seq", split_axis=1, concat_axis=0, tiled=True)
    gated = jnp.einsum(
        "cij,jcd->icd", cross_factor, spread_mixed, preferred_element_type=f32
    ).astype(bf16)
    gated_home = lax.all_to_all(gated, "seq", split_axis=0, concat_axis=1, tiled=True)
    grad_cross = jnp.einsum(
        "icd,jcd->cij", spread_grad, spread_mixed, preferred_element_type=f32
    ) / math.sqrt(width)
    back = jnp.einsum("cij,icd->jcd", cross_factor, spread_grad, preferred_element_type=f32).astype(
        bf16
    )
    back_home = lax.all_to_all(back, "seq", split_axis=0, concat_axis=1, tiled=True)
    grad_gate = (cotangent.astype(f32) * gated_home[0].astype(f32)).astype(bf16)
    back_rows = back_home[0]
    partial_block = lax.dot_general(
        back_rows, permuted, (((1,), (1,)), ((), ())), preferred_element_type=f32
    )
    grad_block = lax.psum(partial_block, "seq") / math.sqrt(count * width)
    spread = lax.dot_general(
        block_factor, back_rows, (((0,), (0,)), ((), ())), preferred_element_type=f32
    ).astype(bf16)
    grad_signal = jnp.zeros_like(spread).at[order_table].set(spread)
    return (grad_signal, grad_gate, grad_block, grad_cross)


def solution(mesh):
    in_specs = (
        P(("groups", "seq"), None),
        P(("groups", "seq"), None),
        P(("groups", "seq"), None),
        P(),
        P("seq", None, None),
        P(),
    )
    out_specs = (
        P(("groups", "seq"), None),
        P(("groups", "seq"), None),
        P("groups", None),
        P("seq", "groups", None),
    )
    return jax.shard_map(
        per_device, mesh=mesh, in_specs=in_specs, out_specs=out_specs, check_vma=False
    )
```

profile of v0, /device:TPU:0, one launch (start us, length us, event | category | flops | bytes accessed | tf_op | source)
XLA Modules:
  0.0 409.7 jit_solution(3647754906035799778)
XLA Ops:
  7.2 0.0 copy-start
  7.2 0.8 compare_and_fusion
  8.0 0.7 compare_select_fusion
  8.7 0.1 copy-done
  8.8 0.0 copy-start.10
  8.8 3.3 gather_fusion
  12.1 0.0 copy-done.10
  12.1 3.1 fusion.3
  15.1 7.7 %copy.32 = bf16[1,512,2048]{2,0,1:T(2,128)(2,1)} copy(bf16[1,512,2048]{1,2,0:T(8,128)(2,1)S(1)} %fusion.3) | data formatting | bytes 4194304 | tf_op jit(solution)/shard_map/broadcast_in_dim | solution.py:16
  22.9 0.5 broadcast.9
  23.4 13.2 %reduce = bf16[512,2048]{1,0:T(8,128)(2,1)S(1)} reduce(bf16[512,1,2048]{2,1,0:T(2,128)(2,1)} %bitcast.31, bf16[]{:T(256)} %broadcast.9), dimensions={1}, to_apply=%bitcast.20.reduce_sub_computation | reduce | bytes 4194306
  36.5 2.8 reshape.52
  39.3 0.0 copy-start.9
  39.3 7.5 %all-to-all-start.2 = ((bf16[16,2,32768]{2,1,0:T(2,128)(2,1)}), bf16[16,2,32768]{2,1,0:T(2,128)(2,1)S(1)}, u32[]{:S(2)}, u32[]{:S(2)}) async-start(bf16[16,2,32768]{2,1,0:T(2,128)(2,1)} %reshape.52), calls=%async_computation.2 | async-start | bytes 4194304 | tf_op jit(solution)/shard_map/all_to_all | solution.py:16
  46.8 0.0 all-reduce.2.cloned.1.call-start
  46.9 0.0 copy-done.9
  46.9 0.2 copy.34
  47.1 40.9 %all-to-all-done.2 = bf16[16,2,32768]{2,1,0:T(2,128)(2,1)S(1)} async-done(((bf16[16,2,32768]{2,1,0:T(2,128)(2,1)}), bf16[16,2,32768]{2,1,0:T(2,128)(2,1)S(1)}, u32[]{:S(2)}, u32[]{:S(2)}) %all-to-all-start.2) | async-done | bytes 2097184 | tf_op jit(solution)/shard_map/all_to_all | solution.py:16
  87.9 6.7 %reshape.53 = bf16[512,1,2048]{2,1,0:T(2,128)(2,1)} reshape(bf16[16,2,32768]{2,1,0:T(2,128)(2,1)S(1)} %all-to-all-done.2) | data formatting | bytes 4194304
  94.7 3.5 copy.40
  98.1 0.0 copy-start.2
  98.1 2.4 fusion.5
  100.6 0.0 copy-done.2
  100.6 1.2 copy.35
  101.7 0.0 copy-start.5
  101.8 0.0 copy-start.6
  101.8 58.6 %all_to_all.42 = bf16[16,32,2048]{2,1,0:T(8,128)(2,1)S(1)} all-to-all(bf16[16,32,2048]{2,1,0:T(8,128)(2,1)S(1)} %copy.35), channel_id=1, replica_groups=mesh['groups'=2,'seq'=16] {'seq'}, dimensions={0} | all-to-all | bytes 4194304 | tf_op jit(solution)/shard_map/all_to_all | solution.py:21
  160.4 0.0 copy-done.5
  160.4 0.0 copy-done.6
  160.4 3.0 fusion.1
  163.3 5.2 %copy.54 = bf16[1,512,2048]{2,0,1:T(2,128)(2,1)} copy(bf16[1,512,2048]{2,1,0:T(8,128)(2,1)S(1)} %get-tuple-element.17) | data formatting | bytes 4194304 | tf_op jit(solution)/shard_map/broadcast_in_dim | solution.py:17
  168.5 13.2 %reduce.1 = bf16[512,2048]{1,0:T(8,128)(2,1)S(1)} reduce(bf16[512,1,2048]{2,1,0:T(2,128)(2,1)} %bitcast.32, bf16[]{:T(256)} %broadcast.9), dimensions={1}, to_apply=%bitcast.29.reduce_sub_computation | reduce | bytes 4194306
  181.7 2.8 reshape.50
  184.4 52.4 %all_to_all.43 = bf16[16,2,32768]{2,1,0:T(2,128)(2,1)S(1)} all-to-all(bf16[16,2,32768]{2,1,0:T(2,128)(2,1)} %reshape.50), channel_id=1, replica_groups=mesh['groups'=2,'seq'=16] {'seq'}, dimensions={0} | all-to-all | bytes 4194304 | tf_op jit(solution)/shard_map/all_to_all | solution.py:17
  236.9 6.7 %reshape.51 = bf16[512,1,2048]{2,1,0:T(2,128)(2,1)} reshape(bf16[16,2,32768]{2,1,0:T(2,128)(2,1)S(1)} %all_to_all.43) | data formatting | bytes 4194304
  243.6 3.5 copy.39
  247.1 0.0 copy-start.4
  247.1 2.4 fusion.4
  249.5 0.0 copy-done.4
  249.5 1.2 copy.30
  250.6 0.0 copy-start.7
  250.7 52.4 %all_to_all.44 = bf16[16,32,2048]{2,1,0:T(8,128)(2,1)S(1)} all-to-all(bf16[16,32,2048]{2,1,0:T(8,128)(2,1)S(1)} %copy.30), channel_id=1, replica_groups=mesh['groups'=2,'seq'=16] {'seq'}, dimensions={0} | all-to-all | bytes 4194304 | tf_op jit(solution)/shard_map/all_to_all | solution.py:28
  303.0 0.0 copy-start.8
  303.0 1.4 copy-done.8
  304.4 0.0 copy-done.7
  304.4 0.0 copy-start.3
  304.4 2.3 fusion.19
  306.7 0.0 all-reduce.2.cloned.1.call-update
  306.7 0.0 copy-done.3
  306.7 3.9 fusion.12
  310.6 0.8 copy.38
  311.5 4.3 %fusion.2 = bf16[512,2048]{0,1:T(8,128)(2,1)} fusion(bf16[512,2048]{1,0:T(8,128)(2,1)} %bitcast.40, bf16[512,512]{1,0:T(8,128)(2,1)S(1)} %copy-done.10), kind=kOutput, calls=%fused_computation.10 | convolution fusion | flops 1074790400 | bytes 4718592 | tf_op jit(solution)/shard_map/dot_general | solution.py:35
  315.8 0.0 copy-start.1
  315.8 4.1 %copy.31 = bf16[512,2048]{1,0:T(8,128)(2,1)} copy(bf16[512,2048]{0,1:T(8,128)(2,1)} %fusion.2) | data formatting | bytes 4194304 | tf_op jit(solution)/shard_map/convert_element_type | solution.py:37
  319.9 6.1 %scatter_custom_fusion = bf16[512,2048]{1,0:T(8,128)(2,1)} fusion(s32[512]{0:T(512)S(1)} %compare_select_fusion, bf16[512,2048]{1,0:T(8,128)(2,1)} %copy.31, bf16[]{:T(256)} %constant.8.clone.1), kind=kCustom, calls=%fused_computation.22 | custom fusion | bytes 2097664 | tf_op jit(solution)/shard_map/scatter | solution.py:38
  326.0 74.5 %all-reduce.2.cloned.1.call-done = f32[512,512]{1,0:T(8,128)} async-done(((f32[512,512]{1,0:T(8,128)}), f32[512,512]{1,0:T(8,128)}) %all-reduce.2.cloned.1.call-update) | async-done | bytes 1048592 | tf_op jit(solution)/shard_map/psum | solution.py:34
  400.6 2.3 broadcast_multiply_fusion
  402.9 0.0 copy-done.1
  (1 shorter events, 0.0 us)
Async XLA Ops:
  7.2 1.6 copy-start
  8.8 3.3 copy-start.10
  39.3 7.6 %copy-start.9 = (bf16[32,16,16]{0,2,1:T(8,128)(2,1)S(1)}, bf16[32,16,16]{0,2,1:T(8,128)(2,1)}, u32[]{:S(2)}) copy-start(bf16[32,16,16]{0,2,1:T(8,128)(2,1)} %param.10) | copy-start | bytes 49156
  39.3 48.6 %all-to-all-start.2 = ((bf16[16,2,32768]{2,1,0:T(2,128)(2,1)}), bf16[16,2,32768]{2,1,0:T(2,128)(2,1)S(1)}, u32[]{:S(2)}, u32[]{:S(2)}) async-start(bf16[16,2,32768]{2,1,0:T(2,128)(2,1)} %reshape.52), calls=%async_computation.2 | async-start | bytes 4194304 | tf_op jit(solution)/shard_map/all_to_all | solution.py:16
  46.8 353.7 %all-reduce.2.cloned.1.call-start = ((), (), s32[]{:S(2)}) async-start(), calls=%async_computation.4 | async-start | bytes 2097152 | tf_op jit(solution)/shard_map/psum | solution.py:34
  98.1 2.4 copy-start.2
  101.7 58.6 %copy-start.5 = (bf16[512,2048]{1,0:T(8,128)(2,1)S(1)}, bf16[512,2048]{1,0:T(8,128)(2,1)}, u32[]{:S(2)}) copy-start(bf16[512,2048]{1,0:T(8,128)(2,1)} %param.8) | copy-start | bytes 6291460
  101.8 58.6 %copy-start.6 = (bf16[512,2048]{1,0:T(8,128)(2,1)S(1)}, bf16[512,2048]{1,0:T(8,128)(2,1)}, u32[]{:S(2)}) copy-start(bf16[512,2048]{1,0:T(8,128)(2,1)} %param.7) | copy-start | bytes 6291460
  247.1 2.4 copy-start.4
  250.6 53.7 %copy-start.7 = (bf16[512,2048]{1,0:T(8,128)(2,1)S(1)}, bf16[512,2048]{1,0:T(8,128)(2,1)}, u32[]{:S(2)}) copy-start(bf16[512,2048]{1,0:T(8,128)(2,1)} %gather_fusion) | copy-start | bytes 6291460
  303.0 1.4 copy-start.8
  304.4 2.4 copy-start.3
  315.8 87.1 %copy-start.1 = (bf16[512,2048]{1,0:T(8,128)(2,1)S(1)}, bf16[512,2048]{1,0:T(8,128)(2,1)}, u32[]{:S(2)}) copy-start(bf16[512,2048]{1,0:T(8,128)(2,1)} %param.6) | copy-start | bytes 6291460
Sparse Core Ops, SparseCore 0:
  306.9 93.6 all-reduce.1
where the time goes:
time: 410 us
  blocking collectives  163 us (40%)
  waiting for transfers between devices  115 us (28%)
  local copies, waits for them, and re-layouts  57.6 us (14%)
  other arithmetic  33.1 us (8%)
  matrix products  18.5 us (5%)
  between operations  14.2 us (3%)
  starting transfers between devices  7.56 us (2%)
    psum x1, waiting for transfers between devices, per_device(): grad_block = lax.psum(partial_block, 'seq') / math.sqrt(count * width)  74.5 us
    all_to_all x1, blocking collectives, per_device(): lax.all_to_all(gated, 'seq', split_axis=0, concat_axis=1, tiled=True)  58.6 us
    all_to_all x1, blocking collectives, per_device(): lax.all_to_all(gate_grad[None], 'seq', split_axis=1, concat_axis=0, tiled...  52.4 us
    all_to_all x1, blocking collectives, per_device(): lax.all_to_all(back, 'seq', split_axis=0, concat_axis=1, tiled=True)  52.4 us
    all_to_all x1, waiting for transfers between devices, per_device(): lax.all_to_all(mixed[None], 'seq', split_axis=1, concat_axis=0, tiled=True)  40.9 us
    unnamed x31, local copies, waits for them, and re-layouts  28.9 us
    unnamed x2, other arithmetic  26.3 us
  transfers between devices with their start and end apart: 2, of which 2 were waited for; matrix products, arithmetic and copies ran while one was open for 5% of the time, Pallas kernels for 0%

commit v1 on v0

--- a/solution.py
+++ b/solution.py
@@ -3,6 +3,18 @@
 import jax.numpy as jnp
 from jax import lax
 from jax.sharding import PartitionSpec as P
+
+
+def split_up(shard, dim, size):
+    lengths = shard.shape
+    tiles = shard.reshape(*lengths[:dim], size, lengths[dim] // size, *lengths[dim + 1 :])
+    return jnp.moveaxis(tiles, dim, 0)
+
+
+def in_order(parts, dim):
+    dims = list(parts.shape[1:])
+    dims[dim] *= parts.shape[0]
+    return jnp.moveaxis(parts, 0, dim).reshape(dims)
 
 
 def per_device(signal, gate_input, cotangent, block_factor, cross_factor, order_table):
@@ -18,7 +30,15 @@
     gated = jnp.einsum(
         "cij,jcd->icd", cross_factor, spread_mixed, preferred_element_type=f32
     ).astype(bf16)
-    gated_home = lax.all_to_all(gated, "seq", split_axis=0, concat_axis=1, tiled=True)
+    count_2, index = (lax.axis_size("seq"), lax.axis_index("seq"))
+    blocks = split_up(gated, 0, count_2)
+    out = blocks
+    for hop in range(1, count_2):
+        target, source = ((index + hop) % count_2, (index - hop) % count_2)
+        sent = lax.dynamic_index_in_dim(blocks, target, 0)
+        other = lax.ppermute(sent, "seq", [(i, (i + hop) % count_2) for i in range(count_2)])
+        out = lax.dynamic_update_slice_in_dim(out, other, source, axis=0)
+    gated_home = in_order(out, 1)
     grad_cross = jnp.einsum(
         "icd,jcd->cij", spread_grad, spread_mixed, preferred_element_type=f32
     ) / math.sqrt(width)

time: 410 us -> 525 us (1.28); the launches traced: 410 us -> 515 us
  local copies, waits for them, and re-layouts: 57.6 us -> 130 us
  blocking collectives: 163 us -> 103 us
  starting transfers between devices: 7.56 us -> 56.5 us
  waiting for transfers between devices: 115 us -> 158 us
    dynamic_update_slice x0 -> x15, local copies, waits for them, and re-layouts: none -> 64.2 us  [per_device(): out = lax.dynamic_update_slice_in_dim(out, other, source, axis=0)]
    all_to_all x1 -> x0, blocking collectives: 58.6 us -> none  [per_device(): lax.all_to_all(gated, 'seq', split_axis=0, concat_axis=1, tiled=True)]
    ppermute x0 -> x15, starting transfers between devices: none -> 48.5 us  [per_device(): lax.ppermute(sent, 'seq', [(i, (i + hop) % count_2) for i in range(count_...]
    ppermute x0 -> x15, waiting for transfers between devices: none -> 43.7 us  [per_device(): lax.ppermute(sent, 'seq', [(i, (i + hop) % count_2) for i in range(count_...]
    unnamed x31 -> x53, local copies, waits for them, and re-layouts: 28.9 us -> 32 us
  transfers between devices with their start and end apart: 2 -> 17, of which waited for: 2 -> 8; matrix products, arithmetic and copies ran while one was open for 5% -> 15% of each run, Pallas kernels for 0% -> 0%
where the time goes in v1:
time: 525 us; the launch traced here: 515 us
  waiting for transfers between devices  158 us (30%)
  local copies, waits for them, and re-layouts  130 us (25%)
  blocking collectives  103 us (20%)
  starting transfers between devices  56.5 us (11%)
  other arithmetic  32.9 us (6%)
  matrix products  18.5 us (4%)
  between operations  15.3 us (3%)
    psum x1, waiting for transfers between devices, per_device(): grad_block = lax.psum(partial_block, 'seq') / math.sqrt(count * width)  74.5 us
    dynamic_update_slice x15, local copies, waits for them, and re-layouts, per_device(): out = lax.dynamic_update_slice_in_dim(out, other, source, axis=0)  64.2 us
    all_to_all x1, blocking collectives, per_device(): lax.all_to_all(back, 'seq', split_axis=0, concat_axis=1, tiled=True)  52.2 us
    all_to_all x1, blocking collectives, per_device(): lax.all_to_all(gate_grad[None], 'seq', split_axis=1, concat_axis=0, tiled...  51.2 us
    ppermute x15, starting transfers between devices, per_device(): lax.ppermute(sent, 'seq', [(i, (i + hop) % count_2) for i in range(count_...  48.5 us
    ppermute x15, waiting for transfers between devices, per_device(): lax.ppermute(sent, 'seq', [(i, (i + hop) % count_2) for i in range(count_...  43.7 us
    all_to_all x1, waiting for transfers between devices, per_device(): lax.all_to_all(mixed[None], 'seq', split_axis=1, concat_axis=0, tiled=True)  40.1 us
    unnamed x53, local copies, waits for them, and re-layouts  32 us
  transfers between devices with their start and end apart: 17, of which 8 were waited for; matrix products, arithmetic and copies ran while one was open for 15% of the time, Pallas kernels for 0%

profile of v1, /device:TPU:0, one launch (start us, length us, event | category | flops | bytes accessed | tf_op | source)
XLA Modules:
  0.0 514.9 jit_solution(10524530545125910067)
XLA Ops:
  7.2 0.8 compare_and_fusion
  8.0 0.7 compare_select_fusion
  8.8 3.3 gather_fusion
  12.1 3.1 fusion.3
  15.1 7.7 %copy.32 = bf16[1,512,2048]{2,0,1:T(2,128)(2,1)} copy(bf16[1,512,2048]{1,2,0:T(8,128)(2,1)S(1)} %fusion.3) | data formatting | bytes 4194304 | tf_op jit(solution)/shard_map/broadcast_in_dim | solution.py:28
  22.9 0.5 broadcast.39
  23.4 13.2 %reduce = bf16[512,2048]{1,0:T(8,128)(2,1)S(1)} reduce(bf16[512,1,2048]{2,1,0:T(2,128)(2,1)} %bitcast.62, bf16[]{:T(256)} %broadcast.39), dimensions={1}, to_apply=%bitcast.48.reduce_sub_computation | reduce | bytes 4194306
  36.5 2.8 reshape.95
  39.3 7.5 %all-to-all-start.2 = ((bf16[16,2,32768]{2,1,0:T(2,128)(2,1)}), bf16[16,2,32768]{2,1,0:T(2,128)(2,1)S(1)}, u32[]{:S(2)}, u32[]{:S(2)}) async-start(bf16[16,2,32768]{2,1,0:T(2,128)(2,1)} %reshape.95), calls=%async_computation.2 | async-start | bytes 4194304 | tf_op jit(solution)/shard_map/all_to_all | solution.py:28
  47.8 40.1 %all-to-all-done.2 = bf16[16,2,32768]{2,1,0:T(2,128)(2,1)S(1)} async-done(((bf16[16,2,32768]{2,1,0:T(2,128)(2,1)}), bf16[16,2,32768]{2,1,0:T(2,128)(2,1)S(1)}, u32[]{:S(2)}, u32[]{:S(2)}) %all-to-all-start.2) | async-done | bytes 2097184 | tf_op jit(solution)/shard_map/all_to_all | solution.py:28
  87.9 6.8 %reshape.96 = bf16[512,1,2048]{2,1,0:T(2,128)(2,1)} reshape(bf16[16,2,32768]{2,1,0:T(2,128)(2,1)S(1)} %all-to-all-done.2) | data formatting | bytes 4194304
  94.7 3.5 copy.40
  98.2 1.4 copy-done.2
  99.5 2.4 convolution_convert_fusion
  102.0 5.0 dynamic-slice_bitcast_fusion
  107.0 8.6 %collective-permute-start.9 = (bf16[1,1,32,2048]{3,0,2,1:T(2,128)(2,1)S(1)}, bf16[1,1,32,2048]{3,0,2,1:T(2,128)(2,1)S(1)}, u32[]{:S(2)}, u32[]{:S(2)}) collective-permute-start(bf16[1,1,32,2048]{3,0,2,1:T(2,128)(2,1)S(1)} %get-tuple-element.23), channel_id=1, source_target_pairs={{0,10},{1,11},{2,12},{3,13},{4,14},{5,15},{6,0},{7,1},{8,2},{9,3},... | collective-permute-start | bytes 393224 | tf_op jit(solution)/shard_map/ppermute | solution.py:39
  115.7 1.8 collective-permute-start.7
  117.5 1.4 collective-permute-start.6
  118.8 3.8 collective-permute-start.5
  123.1 18.6 %collective-permute-start.4 = (bf16[1,1,32,2048]{3,0,2,1:T(2,128)(2,1)S(1)}, bf16[1,1,32,2048]{3,0,2,1:T(2,128)(2,1)S(1)}, u32[]{:S(2)}, u32[]{:S(2)}) collective-permute-start(bf16[1,1,32,2048]{3,0,2,1:T(2,128)(2,1)S(1)} %get-tuple-element.28), channel_id=1, source_target_pairs={{0,5},{1,6},{2,7},{3,8},{4,9},{5,10},{6,11},{7,12},{8,13},{9,14},{... | collective-permute-start | bytes 393224 | tf_op jit(solution)/shard_map/ppermute | solution.py:39
  141.7 13.3 %collective-permute-start.3 = (bf16[1,1,32,2048]{3,0,2,1:T(2,128)(2,1)S(1)}, bf16[1,1,32,2048]{3,0,2,1:T(2,128)(2,1)S(1)}, u32[]{:S(2)}, u32[]{:S(2)}) collective-permute-start(bf16[1,1,32,2048]{3,0,2,1:T(2,128)(2,1)S(1)} %get-tuple-element.29), channel_id=1, source_target_pairs={{0,4},{1,5},{2,6},{3,7},{4,8},{5,9},{6,10},{7,11},{8,12},{9,13},{1... | collective-permute-start | bytes 393224 | tf_op jit(solution)/shard_map/ppermute | solution.py:39
  155.0 19.1 %collective-permute-done.7 = bf16[1,1,32,2048]{3,0,2,1:T(2,128)(2,1)S(1)} collective-permute-done((bf16[1,1,32,2048]{3,0,2,1:T(2,128)(2,1)S(1)}, bf16[1,1,32,2048]{3,0,2,1:T(2,128)(2,1)S(1)}, u32[]{:S(2)}, u32[]{:S(2)}) %collective-permute-start.7) | collective-permute-done | bytes 131104 | tf_op jit(solution)/shard_map/ppermute | solution.py:39
  174.1 1.7 collective-permute-done.6
  175.9 12.0 %collective-permute-done.5 = bf16[1,1,32,2048]{3,0,2,1:T(2,128)(2,1)S(1)} collective-permute-done((bf16[1,1,32,2048]{3,0,2,1:T(2,128)(2,1)S(1)}, bf16[1,1,32,2048]{3,0,2,1:T(2,128)(2,1)S(1)}, u32[]{:S(2)}, u32[]{:S(2)}) %collective-permute-start.5) | collective-permute-done | bytes 131104 | tf_op jit(solution)/shard_map/ppermute | solution.py:39
  187.9 3.0 collective-permute-done.4
  191.1 0.7 collective-permute-start.13
  191.8 7.3 %collective-permute-done = bf16[1,1,32,2048]{3,0,2,1:T(2,128)(2,1)S(1)} collective-permute-done((bf16[1,1,32,2048]{3,0,2,1:T(2,128)(2,1)S(1)}, bf16[1,1,32,2048]{3,0,2,1:T(2,128)(2,1)S(1)}, u32[]{:S(2)}, u32[]{:S(2)}) %collective-permute-start) | collective-permute-done | bytes 131104 | tf_op jit(solution)/shard_map/ppermute | solution.py:39
  199.2 0.6 copy-done.18
  200.3 4.3 dynamic_update_slice.45
  204.6 4.3 dynamic_update_slice.46
  208.9 4.3 dynamic_update_slice.47
  213.2 4.3 dynamic_update_slice.48
  217.5 4.3 dynamic_update_slice.49
  221.7 4.3 dynamic_update_slice.50
  226.0 4.3 dynamic_update_slice.51
  230.3 4.3 dynamic_update_slice.52
  234.6 4.3 dynamic_update_slice.53
  238.9 4.3 dynamic_update_slice.54
  243.2 4.3 dynamic_update_slice.55
  247.5 4.3 dynamic_update_slice.56
  251.8 4.3 dynamic_update_slice.57
  256.1 4.3 dynamic_update_slice.58
  260.4 4.3 dynamic_update_slice.59
  264.7 1.2 copy.35
  266.3 0.6 copy-done.8
  266.9 2.8 fusion.1
  269.7 5.2 %copy.54 = bf16[1,512,2048]{2,0,1:T(2,128)(2,1)} copy(bf16[1,512,2048]{2,1,0:T(8,128)(2,1)S(1)} %get-tuple-element.17) | data formatting | bytes 4194304 | tf_op jit(solution)/shard_map/broadcast_in_dim | solution.py:29
  274.9 13.2 %reduce.1 = bf16[512,2048]{1,0:T(8,128)(2,1)S(1)} reduce(bf16[512,1,2048]{2,1,0:T(2,128)(2,1)} %bitcast.63, bf16[]{:T(256)} %broadcast.39), dimensions={1}, to_apply=%bitcast.59.reduce_sub_computation | reduce | bytes 4194306
  288.0 2.8 reshape.97
  290.8 51.2 %all_to_all.33 = bf16[16,2,32768]{2,1,0:T(2,128)(2,1)S(1)} all-to-all(bf16[16,2,32768]{2,1,0:T(2,128)(2,1)} %reshape.97), channel_id=1, replica_groups=mesh['groups'=2,'seq'=16] {'seq'}, dimensions={0} | all-to-all | bytes 4194304 | tf_op jit(solution)/shard_map/all_to_all | solution.py:29
  342.0 6.8 %reshape.98 = bf16[512,1,2048]{2,1,0:T(2,128)(2,1)} reshape(bf16[16,2,32768]{2,1,0:T(2,128)(2,1)S(1)} %all_to_all.33) | data formatting | bytes 4194304
  348.7 3.5 copy.39
  352.2 2.4 fusion.4
  354.6 1.2 copy.30
  355.8 52.2 %all_to_all.34 = bf16[16,32,2048]{2,1,0:T(8,128)(2,1)S(1)} all-to-all(bf16[16,32,2048]{2,1,0:T(8,128)(2,1)S(1)} %copy.30), channel_id=1, replica_groups=mesh['groups'=2,'seq'=16] {'seq'}, dimensions={0} | all-to-all | bytes 4194304 | tf_op jit(solution)/shard_map/all_to_all | solution.py:48
  408.0 1.4 copy-done.6
  409.3 2.3 fusion.18
  411.7 4.0 fusion.11
  415.7 0.8 copy.38
  416.5 4.3 fusion.2
  420.8 4.1 copy.31
  424.9 6.1 %scatter_custom_fusion = bf16[512,2048]{1,0:T(8,128)(2,1)} fusion(s32[512]{0:T(512)S(1)} %compare_select_fusion, bf16[512,2048]{1,0:T(8,128)(2,1)} %copy.31, bf16[]{:T(256)} %constant.211.clone.1), kind=kCustom, calls=%fused_computation.21 | custom fusion | bytes 2097664 | tf_op jit(solution)/shard_map/scatter | solution.py:58
  431.1 74.5 %all-reduce.2.cloned.1.call-done = f32[512,512]{1,0:T(8,128)} async-done(((f32[512,512]{1,0:T(8,128)}), f32[512,512]{1,0:T(8,128)}) %all-reduce.2.cloned.1.call-update) | async-done | bytes 1048592 | tf_op jit(solution)/shard_map/psum | solution.py:54
  505.5 2.3 broadcast_multiply_fusion
  (62 shorter events, 2.1 us)
Async XLA Ops:
  7.2 1.6 copy-start
  8.8 3.3 copy-start.20
  39.3 8.2 %copy-start.19 = (bf16[32,16,16]{0,2,1:T(8,128)(2,1)S(1)}, bf16[32,16,16]{0,2,1:T(8,128)(2,1)}, u32[]{:S(2)}) copy-start(bf16[32,16,16]{0,2,1:T(8,128)(2,1)} %param.10) | copy-start | bytes 49156
  39.3 48.6 %all-to-all-start.2 = ((bf16[16,2,32768]{2,1,0:T(2,128)(2,1)}), bf16[16,2,32768]{2,1,0:T(2,128)(2,1)S(1)}, u32[]{:S(2)}, u32[]{:S(2)}) async-start(bf16[16,2,32768]{2,1,0:T(2,128)(2,1)} %reshape.95), calls=%async_computation.2 | async-start | bytes 4194304 | tf_op jit(solution)/shard_map/all_to_all | solution.py:28
  46.8 458.7 %all-reduce.2.cloned.1.call-start = ((), (), s32[]{:S(2)}) async-start(), calls=%async_computation.3 | async-start | bytes 2097152 | tf_op jit(solution)/shard_map/psum | solution.py:54
  98.2 1.4 copy-start.2
  107.0 16.1 %collective-permute-start.9 = (bf16[1,1,32,2048]{3,0,2,1:T(2,128)(2,1)S(1)}, bf16[1,1,32,2048]{3,0,2,1:T(2,128)(2,1)S(1)}, u32[]{:S(2)}, u32[]{:S(2)}) collective-permute-start(bf16[1,1,32,2048]{3,0,2,1:T(2,128)(2,1)S(1)} %get-tuple-element.23), channel_id=1, source_target_pairs={{0,10},{1,11},{2,12},{3,13},{4,14},{5,15},{6,0},{7,1},{8,2},{9,3},... | collective-permute-start | bytes 393224 | tf_op jit(solution)/shard_map/ppermute | solution.py:39
  115.6 26.2 %collective-permute-start.8 = (bf16[1,1,32,2048]{3,0,2,1:T(2,128)(2,1)S(1)}, bf16[1,1,32,2048]{3,0,2,1:T(2,128)(2,1)S(1)}, u32[]{:S(2)}, u32[]{:S(2)}) collective-permute-start(bf16[1,1,32,2048]{3,0,2,1:T(2,128)(2,1)S(1)} %get-tuple-element.24), channel_id=1, source_target_pairs={{0,9},{1,10},{2,11},{3,12},{4,13},{5,14},{6,15},{7,0},{8,1},{9,2},... | collective-permute-start | bytes 393224 | tf_op jit(solution)/shard_map/ppermute | solution.py:39
  115.7 58.4 %collective-permute-start.7 = (bf16[1,1,32,2048]{3,0,2,1:T(2,128)(2,1)S(1)}, bf16[1,1,32,2048]{3,0,2,1:T(2,128)(2,1)S(1)}, u32[]{:S(2)}, u32[]{:S(2)}) collective-permute-start(bf16[1,1,32,2048]{3,0,2,1:T(2,128)(2,1)S(1)} %get-tuple-element.25), channel_id=1, source_target_pairs={{0,8},{1,9},{2,10},{3,11},{4,12},{5,13},{6,14},{7,15},{8,0},{9,1},... | collective-permute-start | bytes 393224 | tf_op jit(solution)/shard_map/ppermute | solution.py:39
  117.5 58.4 %collective-permute-start.6 = (bf16[1,1,32,2048]{3,0,2,1:T(2,128)(2,1)S(1)}, bf16[1,1,32,2048]{3,0,2,1:T(2,128)(2,1)S(1)}, u32[]{:S(2)}, u32[]{:S(2)}) collective-permute-start(bf16[1,1,32,2048]{3,0,2,1:T(2,128)(2,1)S(1)} %get-tuple-element.26), channel_id=1, source_target_pairs={{0,7},{1,8},{2,9},{3,10},{4,11},{5,12},{6,13},{7,14},{8,15},{9,0},... | collective-permute-start | bytes 393224 | tf_op jit(solution)/shard_map/ppermute | solution.py:39
  118.8 69.1 %collective-permute-start.5 = (bf16[1,1,32,2048]{3,0,2,1:T(2,128)(2,1)S(1)}, bf16[1,1,32,2048]{3,0,2,1:T(2,128)(2,1)S(1)}, u32[]{:S(2)}, u32[]{:S(2)}) collective-permute-start(bf16[1,1,32,2048]{3,0,2,1:T(2,128)(2,1)S(1)} %get-tuple-element.27), channel_id=1, source_target_pairs={{0,6},{1,7},{2,8},{3,9},{4,10},{5,11},{6,12},{7,13},{8,14},{9,15},... | collective-permute-start | bytes 393224 | tf_op jit(solution)/shard_map/ppermute | solution.py:39
  123.1 76.0 %copy-start.9 = (bf16[1,1,32,2048]{3,0,2,1:T(2,128)(2,1)}, bf16[1,1,32,2048]{3,0,2,1:T(2,128)(2,1)S(1)}, u32[]{:S(2)}) copy-start(bf16[1,1,32,2048]{3,0,2,1:T(2,128)(2,1)S(1)} %collective-permute-done.9) | copy-start | bytes 393220
  123.1 67.8 %collective-permute-start.4 = (bf16[1,1,32,2048]{3,0,2,1:T(2,128)(2,1)S(1)}, bf16[1,1,32,2048]{3,0,2,1:T(2,128)(2,1)S(1)}, u32[]{:S(2)}, u32[]{:S(2)}) collective-permute-start(bf16[1,1,32,2048]{3,0,2,1:T(2,128)(2,1)S(1)} %get-tuple-element.28), channel_id=1, source_target_pairs={{0,5},{1,6},{2,7},{3,8},{4,9},{5,10},{6,11},{7,12},{8,13},{9,14},{... | collective-permute-start | bytes 393224 | tf_op jit(solution)/shard_map/ppermute | solution.py:39
  141.7 57.4 %copy-start.10 = (bf16[1,1,32,2048]{3,0,2,1:T(2,128)(2,1)}, bf16[1,1,32,2048]{3,0,2,1:T(2,128)(2,1)S(1)}, u32[]{:S(2)}) copy-start(bf16[1,1,32,2048]{3,0,2,1:T(2,128)(2,1)S(1)} %collective-permute-done.8) | copy-start | bytes 393220
  141.7 49.2 %collective-permute-start.3 = (bf16[1,1,32,2048]{3,0,2,1:T(2,128)(2,1)S(1)}, bf16[1,1,32,2048]{3,0,2,1:T(2,128)(2,1)S(1)}, u32[]{:S(2)}, u32[]{:S(2)}) collective-permute-start(bf16[1,1,32,2048]{3,0,2,1:T(2,128)(2,1)S(1)} %get-tuple-element.29), channel_id=1, source_target_pairs={{0,4},{1,5},{2,6},{3,7},{4,8},{5,9},{6,10},{7,11},{8,12},{9,13},{1... | collective-permute-start | bytes 393224 | tf_op jit(solution)/shard_map/ppermute | solution.py:39
  174.1 25.0 %copy-start.11 = (bf16[1,1,32,2048]{3,0,2,1:T(2,128)(2,1)}, bf16[1,1,32,2048]{3,0,2,1:T(2,128)(2,1)S(1)}, u32[]{:S(2)}) copy-start(bf16[1,1,32,2048]{3,0,2,1:T(2,128)(2,1)S(1)} %collective-permute-done.7) | copy-start | bytes 393220
  174.1 16.9 %collective-permute-start.2 = (bf16[1,1,32,2048]{3,0,2,1:T(2,128)(2,1)S(1)}, bf16[1,1,32,2048]{3,0,2,1:T(2,128)(2,1)S(1)}, u32[]{:S(2)}, u32[]{:S(2)}) collective-permute-start(bf16[1,1,32,2048]{3,0,2,1:T(2,128)(2,1)S(1)} %get-tuple-element.30), channel_id=1, source_target_pairs={{0,3},{1,4},{2,5},{3,6},{4,7},{5,8},{6,9},{7,10},{8,11},{9,12},{10... | collective-permute-start | bytes 393224 | tf_op jit(solution)/shard_map/ppermute | solution.py:39
  175.9 23.3 %copy-start.12 = (bf16[1,1,32,2048]{3,0,2,1:T(2,128)(2,1)}, bf16[1,1,32,2048]{3,0,2,1:T(2,128)(2,1)S(1)}, u32[]{:S(2)}) copy-start(bf16[1,1,32,2048]{3,0,2,1:T(2,128)(2,1)S(1)} %collective-permute-done.6) | copy-start | bytes 393220
  175.9 15.2 %collective-permute-start.1 = (bf16[1,1,32,2048]{3,0,2,1:T(2,128)(2,1)S(1)}, bf16[1,1,32,2048]{3,0,2,1:T(2,128)(2,1)S(1)}, u32[]{:S(2)}, u32[]{:S(2)}) collective-permute-start(bf16[1,1,32,2048]{3,0,2,1:T(2,128)(2,1)S(1)} %get-tuple-element.31), channel_id=1, source_target_pairs={{0,2},{1,3},{2,4},{3,5},{4,6},{5,7},{6,8},{7,9},{8,10},{9,11},{10,... | collective-permute-start | bytes 393224 | tf_op jit(solution)/shard_map/ppermute | solution.py:39
  187.9 11.2 %copy-start.13 = (bf16[1,1,32,2048]{3,0,2,1:T(2,128)(2,1)}, bf16[1,1,32,2048]{3,0,2,1:T(2,128)(2,1)S(1)}, u32[]{:S(2)}) copy-start(bf16[1,1,32,2048]{3,0,2,1:T(2,128)(2,1)S(1)} %collective-permute-done.5) | copy-start | bytes 393220
  187.9 11.2 %collective-permute-start = (bf16[1,1,32,2048]{3,0,2,1:T(2,128)(2,1)S(1)}, bf16[1,1,32,2048]{3,0,2,1:T(2,128)(2,1)S(1)}, u32[]{:S(2)}, u32[]{:S(2)}) collective-permute-start(bf16[1,1,32,2048]{3,0,2,1:T(2,128)(2,1)S(1)} %get-tuple-element.32), channel_id=1, source_target_pairs={{0,1},{1,2},{2,3},{3,4},{4,5},{5,6},{6,7},{7,8},{8,9},{9,10},{10,1... | collective-permute-start | bytes 393224 | tf_op jit(solution)/shard_map/ppermute | solution.py:39
  190.9 8.3 %copy-start.14 = (bf16[1,1,32,2048]{3,0,2,1:T(2,128)(2,1)}, bf16[1,1,32,2048]{3,0,2,1:T(2,128)(2,1)S(1)}, u32[]{:S(2)}) copy-start(bf16[1,1,32,2048]{3,0,2,1:T(2,128)(2,1)S(1)} %collective-permute-done.4) | copy-start | bytes 393220
  190.9 60.9 %collective-permute-start.12 = (bf16[1,1,32,2048]{3,0,2,1:T(2,128)(2,1)S(1)}, bf16[1,1,32,2048]{3,0,2,1:T(2,128)(2,1)}, u32[]{:S(2)}, u32[]{:S(2)}) collective-permute-start(bf16[1,1,32,2048]{3,0,2,1:T(2,128)(2,1)S(1)} %get-tuple-element.20), channel_id=1, source_target_pairs={{0,13},{1,14},{2,15},{3,0},{4,1},{5,2},{6,3},{7,4},{8,5},{9,6},{10... | collective-permute-start | bytes 393224 | tf_op jit(solution)/shard_map/ppermute | solution.py:39
  190.9 8.3 %copy-start.15 = (bf16[1,1,32,2048]{3,0,2,1:T(2,128)(2,1)}, bf16[1,1,32,2048]{3,0,2,1:T(2,128)(2,1)S(1)}, u32[]{:S(2)}) copy-start(bf16[1,1,32,2048]{3,0,2,1:T(2,128)(2,1)S(1)} %collective-permute-done.3) | copy-start | bytes 393220
  190.9 52.3 %collective-permute-start.10 = (bf16[1,1,32,2048]{3,0,2,1:T(2,128)(2,1)S(1)}, bf16[1,1,32,2048]{3,0,2,1:T(2,128)(2,1)}, u32[]{:S(2)}, u32[]{:S(2)}) collective-permute-start(bf16[1,1,32,2048]{3,0,2,1:T(2,128)(2,1)S(1)} %get-tuple-element.22), channel_id=1, source_target_pairs={{0,11},{1,12},{2,13},{3,14},{4,15},{5,0},{6,1},{7,2},{8,3},{9,4},{... | collective-permute-start | bytes 393224 | tf_op jit(solution)/shard_map/ppermute | solution.py:39
  191.0 8.2 %copy-start.16 = (bf16[1,1,32,2048]{3,0,2,1:T(2,128)(2,1)}, bf16[1,1,32,2048]{3,0,2,1:T(2,128)(2,1)S(1)}, u32[]{:S(2)}) copy-start(bf16[1,1,32,2048]{3,0,2,1:T(2,128)(2,1)S(1)} %collective-permute-done.2) | copy-start | bytes 393220
  191.0 56.5 %collective-permute-start.11 = (bf16[1,1,32,2048]{3,0,2,1:T(2,128)(2,1)S(1)}, bf16[1,1,32,2048]{3,0,2,1:T(2,128)(2,1)}, u32[]{:S(2)}, u32[]{:S(2)}) collective-permute-start(bf16[1,1,32,2048]{3,0,2,1:T(2,128)(2,1)S(1)} %get-tuple-element.21), channel_id=1, source_target_pairs={{0,12},{1,13},{2,14},{3,15},{4,0},{5,1},{6,2},{7,3},{8,4},{9,5},{1... | collective-permute-start | bytes 393224 | tf_op jit(solution)/shard_map/ppermute | solution.py:39
  191.1 8.1 %copy-start.17 = (bf16[1,1,32,2048]{3,0,2,1:T(2,128)(2,1)}, bf16[1,1,32,2048]{3,0,2,1:T(2,128)(2,1)S(1)}, u32[]{:S(2)}) copy-start(bf16[1,1,32,2048]{3,0,2,1:T(2,128)(2,1)S(1)} %collective-permute-done.1) | copy-start | bytes 393220
  191.1 65.0 %collective-permute-start.13 = (bf16[1,1,32,2048]{3,0,2,1:T(2,128)(2,1)S(1)}, bf16[1,1,32,2048]{3,0,2,1:T(2,128)(2,1)}, u32[]{:S(2)}, u32[]{:S(2)}) collective-permute-start(bf16[1,1,32,2048]{3,0,2,1:T(2,128)(2,1)S(1)} %get-tuple-element.19), channel_id=1, source_target_pairs={{0,14},{1,15},{2,0},{3,1},{4,2},{5,3},{6,4},{7,5},{8,6},{9,7},{10,... | collective-permute-start | bytes 393224 | tf_op jit(solution)/shard_map/ppermute | solution.py:39
  199.1 0.7 copy-start.18
  199.8 60.6 %collective-permute-start.14 = (bf16[1,1,32,2048]{3,0,2,1:T(2,128)(2,1)S(1)}, bf16[1,1,32,2048]{3,0,2,1:T(2,128)(2,1)}, u32[]{:S(2)}, u32[]{:S(2)}) collective-permute-start(bf16[1,1,32,2048]{3,0,2,1:T(2,128)(2,1)S(1)} %get-tuple-element.18), channel_id=1, source_target_pairs={{0,15},{1,0},{2,1},{3,2},{4,3},{5,4},{6,5},{7,6},{8,7},{9,8},{10,9... | collective-permute-start | bytes 393224 | tf_op jit(solution)/shard_map/ppermute | solution.py:39
  264.7 1.6 copy-start.7
  264.7 2.2 copy-start.8
  352.2 2.4 copy-start.4
  355.8 53.5 %copy-start.5 = (bf16[512,2048]{1,0:T(8,128)(2,1)S(1)}, bf16[512,2048]{1,0:T(8,128)(2,1)}, u32[]{:S(2)}) copy-start(bf16[512,2048]{1,0:T(8,128)(2,1)} %gather_fusion) | copy-start | bytes 6291460
  408.0 1.4 copy-start.6
  409.3 2.4 copy-start.3
  411.7 4.8 copy-start.21
  420.8 87.1 %copy-start.1 = (bf16[512,2048]{1,0:T(8,128)(2,1)S(1)}, bf16[512,2048]{1,0:T(8,128)(2,1)}, u32[]{:S(2)}) copy-start(bf16[512,2048]{1,0:T(8,128)(2,1)} %param.6) | copy-start | bytes 6291460
Sparse Core Ops, SparseCore 0:
  411.8 93.6 all-reduce.1
